TPU v7x, 32 devices: a whole 2x2x4 slice. The times are simulated.
32 devices in a mesh: tm: 2 (over x), space: 16 (over z, y, core).
Axes of the slice: x: 2, y: 2, z: 4, core: 2. Of those that a mesh axis runs over, the one named last changes fastest.
Arguments:
- increment: float32 [4, 5, 48, 128, 128], P('tm', None, None, 'space'), may hold values from -6 to 6
- multiplier: float32 [4, 5, 48, 128, 128], P('tm', None, None, 'space'), may hold values from -20 to 20
- sensor_multiplier: float32 [4, 2048], P('tm'), may hold values from -6 to 6
- misfit: float32 [4, 5, 48, 128, 128], P('tm', None, None, 'space'), may hold values from -20 to 20
- innovation: float32 [4, 2048], P('tm'), may hold values from -6 to 6
- model_error: float32 [5, 48], replicated, may hold values from 0.2 to 1
- sensor_error: float32 [4, 2048], P('tm'), may hold values from 0.3 to 1.5
- trajectory: bfloat16 [4, 2, 2, 48, 128, 128], P('tm', None, None, None, 'space'), may hold values from 0 to 1
- land_sea: int32 [128, 128], P('space'), may hold values 0 or 1
- sensor_cells: int32 [4, 2048], P('tm'), may hold values from 0 to 1572863
Outputs:
- increment_next: float32 [4, 5, 48, 128, 128], P('tm', None, None, 'space')
- multiplier_next: float32 [4, 5, 48, 128, 128], P('tm', None, None, 'space')
- sensor_next: float32 [4, 2048], P('tm')
Inputs may be any that keep to these rules, and one draw needn't show every extreme that they name: `sensor_cells`: the flat index ((f * 48 + l) * 128 + x) * 128 + y of the observed cell at field f (0 temperature, 1 salinity), level l, column x, row y; an index may repeat.
All inputs are finite; a program needn't handle non-finite values. No bound on the sum of `land_sea` on one device may be relied on, other than what follows from the above.
Results may differ from a plain program's by a relative error of at most 0.0017.
Values may be sent and summed in bfloat16 or wider, within the bound.
No kernel may reach another device: no remote copies, remote signals or barrier semaphores. Data moves between devices by JAX's collectives and lax.ppermute only.
A program may use at most 64 MiB of HBM per device.

v0:
```python
import jax
import jax.numpy as jnp
from jax import lax
from jax.sharding import PartitionSpec as P

thermal_lin = 0.2
thermal_quad = 0.02
haline_lin = 0.8
cabbeling = 0.01
gravity = 1.0
time_stride = 0.3
mixing = 0.15
coriolis = 0.5
relaxation = 0.5
epsilon = 1e-06


def extended(shard, sides, width):
    for axis, dim in sides:
        peers, length = (lax.axis_size(axis), shard.shape[dim])
        up = [(i, (i + 1) % peers) for i in range(peers)]
        down = [(j, i) for i, j in up]
        last = lax.slice_in_dim(shard, length - width, length, axis=dim)
        first = lax.slice_in_dim(shard, 0, width, axis=dim)
        before = lax.ppermute(last, axis, up)
        after = lax.ppermute(first, axis, down)
        shard = jnp.concatenate([before, shard, after], axis=dim)
    return shard


def shifted(shard, axis, by):
    peers = lax.axis_size(axis)
    pairs = [(i, i + by) for i in range(peers) if 0 <= i + by < peers]
    return lax.ppermute(shard, axis, pairs)


def column_pad(values):
    return jnp.pad(values, ((0, 0), (0, 0), (1, 1)))


def tendency(padded, history, landmask):
    temper = 30.0 * history[0] - 10.0
    saline = 8.0 * history[1] - 5.0
    dens_temper = -thermal_lin - thermal_quad * temper + cabbeling * saline
    dens_saline = haline_lin + cabbeling * temper
    density = dens_temper * padded[0] + dens_saline * padded[1]
    pressure = padded[4] + gravity * density
    latitude = padded.shape[3]
    rotation = (
        coriolis
        * (jnp.arange(latitude, dtype=jnp.float32) - 0.5 * (latitude - 1))
        / (0.5 * latitude)
    )

    def middle(f):
        return f[:, 1:-1]

    def zonal_slope(f):
        return 0.5 * (f[:, 2:] - f[:, :-2])

    def meridional_slope(f):
        g = column_pad(middle(f))
        return 0.5 * (g[..., 2:] - g[..., :-2])

    def laplacian(f):
        g = column_pad(middle(f))
        return f[:, 2:] + f[:, :-2] + g[..., 2:] + g[..., :-2] - 4.0 * middle(f)

    heat_next = middle(padded[0]) + mixing * laplacian(padded[0])
    salt_next = middle(padded[1]) + mixing * laplacian(padded[1])
    east_next = middle(padded[2]) + time_stride * (
        rotation * middle(padded[3]) - zonal_slope(pressure)
    )
    north_next = middle(padded[3]) + time_stride * (
        -rotation * middle(padded[2]) - meridional_slope(pressure)
    )
    surface_next = (
        middle(padded[4])
        - time_stride * (zonal_slope(padded[2]) + meridional_slope(padded[3]))
        + mixing * laplacian(padded[4])
    )
    return jnp.stack([heat_next, salt_next, east_next, north_next, surface_next]) * landmask


def tangent_substep(fields, history, landmask):
    padded = extended(fields, (("space", 2),), 1)
    return tendency(padded, history, landmask)


def adjoint_substep(upstream, history, landmask):
    blank = jnp.zeros(
        upstream.shape[:2] + (upstream.shape[2] + 2,) + upstream.shape[3:], jnp.float32
    )
    _, pull = jax.vjp(lambda v: tendency(v, history, landmask), blank)
    spread = pull(upstream)[0]
    rims = jnp.concatenate([spread[:, :, :1], spread[:, :, -1:]], axis=2)
    beyond = extended(rims.astype(jnp.bfloat16), (("space", 2),), 1).astype(rims.dtype)
    inner = spread[:, :, 1:-1]
    inner = inner.at[:, :, 0].add(beyond[:, :, 0])
    inner = inner.at[:, :, -1].add(beyond[:, :, 3])
    return inner


def on_device(
    increment,
    multiplier,
    sensor_multiplier,
    misfit,
    innovation,
    model_error,
    sensor_error,
    trajectory,
    land_sea,
    sensor_cells,
):
    subcount = increment.shape[0]
    substeps = trajectory.shape[1]
    levels = increment.shape[2]
    width = increment.shape[3]
    latitude = increment.shape[4]
    landmask = land_sea.astype(jnp.float32)
    forward = []
    history = extended(trajectory, (("space", 4),), 1).astype(jnp.float32)
    for k in range(subcount):
        fields = increment[k]
        for j in range(substeps):
            fields = tangent_substep(fields, history[k, j], landmask)
        forward.append(fields)
    damping = model_error[:, :, None, None]
    partial_value = multiplier[0] + relaxation * (
        misfit[0] - damping * multiplier[0] - increment[0]
    )
    received = shifted(partial_value, "tm", -1)
    incoming = shifted(forward[-1].astype(jnp.bfloat16), "tm", 1).astype(jnp.float32)
    previous = jnp.stack([incoming] + forward[:-1])
    model_residual = misfit - damping[None] * multiplier - (increment - previous)
    multiplier_next = multiplier + relaxation * model_residual
    columns = width * lax.axis_size("space")
    plane = columns * latitude
    offset = lax.axis_index("space") * width
    field_level = sensor_cells // plane
    remainder = sensor_cells % plane
    column_index = remainder // latitude
    row_index = remainder % latitude
    owned = (column_index >= offset) & (column_index < offset + width)
    local_index = jnp.where(
        owned, (field_level * width + (column_index - offset)) * latitude + row_index, 0
    )
    flattened = increment[:, :2].reshape(subcount, 2 * levels * width * latitude)
    local_values = jnp.where(owned, jnp.take_along_axis(flattened, local_index, axis=1), 0.0)
    observed = lax.psum(local_values, "space")
    sensor_residual = innovation - sensor_error * sensor_multiplier - observed
    sensor_next = sensor_multiplier + relaxation * sensor_residual
    misfit_local = jnp.sum(model_residual * model_residual) + jnp.sum(
        jnp.where(owned, sensor_residual * sensor_residual, 0.0)
    )
    misfit_square = lax.psum(misfit_local, ("tm", "space"))
    keeper = jnp.where(lax.axis_index("tm") < lax.axis_size("tm") - 1, 1.0, 0.0).astype(jnp.float32)
    carried = keeper * (received + relaxation * forward[-1])
    following = [multiplier_next[1]] + [carried]
    returned = []
    for k in range(subcount):
        upstream = following[k]
        for j in reversed(range(substeps)):
            upstream = adjoint_substep(upstream, history[k, j], landmask)
        returned.append(upstream)
    returned = jnp.stack(returned)
    subwindow_rows = jnp.arange(subcount, dtype=jnp.int32)[:, None]
    spread = (
        jnp.zeros_like(flattened)
        .at[subwindow_rows, local_index]
        .add(jnp.where(owned, sensor_next, 0.0))
    )
    spread = spread.reshape(subcount, 2, levels, width, latitude)
    sensor_part = jnp.concatenate(
        [spread, jnp.zeros((subcount, 3, levels, width, latitude), jnp.float32)], axis=1
    )
    gradient = multiplier_next - returned + sensor_part
    gradient_local = jnp.sum(gradient * gradient)
    gradient_square = lax.psum(gradient_local, ("tm", "space"))
    stride = misfit_square / (gradient_square + epsilon)
    return (increment - stride * gradient, multiplier_next, sensor_next)


def solution(mesh):
    placed = (
        P("tm", None, None, "space", None),
        P("tm", None, None, "space", None),
        P("tm", None),
        P("tm", None, None, "space", None),
        P("tm", None),
        P(),
        P("tm", None),
        P("tm", None, None, None, "space", None),
        P("space", None),
        P("tm", None),
    )
    return jax.shard_map(
        on_device,
        mesh=mesh,
        in_specs=placed,
        out_specs=(
            P("tm", None, None, "space", None),
            P("tm", None, None, "space", None),
            P("tm", None),
        ),
        check_vma=False,
    )
```

profile of v0, /device:TPU:12, one launch (start us, length us, event | category | flops | bytes accessed | tf_op | source)
XLA Modules:
  0.0 275.0 jit_solution(7733373252977561746)
XLA Ops:
  0.6 1.9 copy.36
  4.5 1.7 collective-permute-start.1
  7.2 2.6 collective-permute-start.2
  10.7 34.9 %gather_fusion = f32[4096]{0:T(1024)S(1)} fusion(f32[2,98304]{1,0:T(2,128)S(1)} %bitcast.526, s32[4096]{0:T(1024)S(1)} %bitcast.527), kind=kCustom, calls=%fused_computation | custom fusion | bytes 65536 | tf_op jit(solution)/shard_map/jit(take_along_axis)/gather | solution.py:150
  45.7 50.0 %psum.21 = f32[2,2048]{1,0:T(2,128)S(1)} all-reduce(f32[2,2048]{1,0:T(2,128)S(1)} %fusion.203), channel_id=1, replica_groups=mesh['tm'=2,'space'=16] {'space'}, use_global_device_ids=true, to_apply=%region_1.2 | all-reduce | flops 4096 | bytes 32768 | tf_op jit(solution)/shard_map/psum | solution.py:151
  95.6 1.3 select_bitcast_fusion.1
  97.2 27.9 %scatter_custom_fusion = f32[196608]{0:T(1024)} fusion(s32[4096]{0:T(1024)S(1)} %bitcast.541, f32[4096]{0:T(1024)S(1)} %bitcast.540, f32[]{:T(128)} %constant.307.clone.1), kind=kCustom, calls=%fused_computation.80 | custom fusion | flops 4096 | bytes 786436
  127.0 1.1 pad_maximum_fusion
  131.9 4.5 %collective-permute-start.5 = (f32[5,48,1,128]{3,1,2,0:T(8,128)S(1)}, f32[5,48,1,128]{3,1,2,0:T(8,128)S(1)}, u32[]{:S(2)}, u32[]{:S(2)}) collective-permute-start(f32[5,48,1,128]{3,1,2,0:T(8,128)S(1)} %get-tuple-element.230), channel_id=1, source_target_pairs={{1,0},{2,1},{3,2},{4,3},{5,4},{6,5},{7,6},{8,7},{9,8},{10,9},{11,1... | collective-permute-start | bytes 368648 | tf_op jit(solution)/shard_map/ppermute | solution.py:26
  137.1 2.9 %collective-permute-done.4 = f32[5,48,1,128]{3,1,2,0:T(8,128)S(1)} collective-permute-done((f32[5,48,1,128]{3,1,2,0:T(8,128)S(1)}, f32[5,48,1,128]{3,1,2,0:T(8,128)S(1)}, u32[]{:S(2)}, u32[]{:S(2)}) %collective-permute-start.4) | collective-permute-done | bytes 122912 | tf_op jit(solution)/shard_map/ppermute | solution.py:25
  140.2 4.0 %collective-permute-done.9 = f32[5,48,1,128]{3,1,2,0:T(8,128)S(1)} collective-permute-done((f32[5,48,1,128]{3,1,2,0:T(8,128)S(1)}, f32[5,48,1,128]{3,1,2,0:T(8,128)S(1)}, u32[]{:S(2)}, u32[]{:S(2)}) %collective-permute-start.9) | collective-permute-done | bytes 122912 | tf_op jit(solution)/shard_map/ppermute | solution.py:25
  145.7 4.3 %collective-permute-start.6 = (bf16[5,48,8,128]{3,1,2,0:T(8,128)(2,1)S(1)}, bf16[5,48,8,128]{3,1,2,0:T(8,128)(2,1)S(1)}, u32[]{:S(2)}, u32[]{:S(2)}) collective-permute-start(bf16[5,48,8,128]{3,1,2,0:T(8,128)(2,1)S(1)} %multiply_convert_fusion), channel_id=1, source_target_pairs={{0,16},{1,17},{2,18},{3,19},{4,20},{5,21},{6,22},{7,23},{8,24},{9,... | collective-permute-start | bytes 1474568 | tf_op jit(solution)/shard_map/ppermute | solution.py:34
  151.1 5.0 %collective-permute-done.6 = bf16[5,48,8,128]{3,1,2,0:T(8,128)(2,1)S(1)} collective-permute-done((bf16[5,48,8,128]{3,1,2,0:T(8,128)(2,1)S(1)}, bf16[5,48,8,128]{3,1,2,0:T(8,128)(2,1)S(1)}, u32[]{:S(2)}, u32[]{:S(2)}) %collective-permute-start.6) | collective-permute-done | bytes 491552 | tf_op jit(solution)/shard_map/ppermute | solution.py:34
  156.2 1.6 broadcast_multiply_fusion
  160.3 1.4 copy-done.4
  161.8 1.2 fusion.5
  163.0 1.3 collective-permute-start.15
  165.8 1.7 collective-permute-start.12
  167.5 1.2 multiply_reduce_fusion.1
  171.1 1.6 fusion.200
  172.7 1.6 fusion.199
  174.2 8.5 %collective-permute-done.15 = f32[5,48,8,128]{3,1,2,0:T(8,128)} collective-permute-done((f32[5,48,8,128]{3,1,2,0:T(8,128)}, f32[5,48,8,128]{3,1,2,0:T(8,128)}, u32[]{:S(2)}, u32[]{:S(2)}) %collective-permute-start.15) | collective-permute-done | bytes 983072 | tf_op jit(solution)/shard_map/ppermute | solution.py:34
  182.7 1.7 broadcast_multiply_fusion.3
  188.1 1.7 collective-permute-start.17
  190.4 7.8 %collective-permute-start.13 = (bf16[5,48,1,128]{3,1,2,0:T(8,128)(2,1)S(1)}, bf16[5,48,1,128]{3,1,2,0:T(8,128)(2,1)S(1)}, u32[]{:S(2)}, u32[]{:S(2)}) collective-permute-start(bf16[5,48,1,128]{3,1,2,0:T(8,128)(2,1)S(1)} %get-tuple-element.239), channel_id=1, source_target_pairs={{0,1},{1,2},{2,3},{3,4},{4,5},{5,6},{6,7},{7,8},{8,9},{9,10},{10,1... | collective-permute-start | bytes 184328 | tf_op jit(solution)/shard_map/ppermute | solution.py:25
  199.1 2.5 collective-permute-done.14
  203.2 4.1 %collective-permute-start.18 = (bf16[5,48,1,128]{3,1,0,2:T(8,128)(2,1)S(1)}, bf16[5,48,1,128]{3,1,0,2:T(8,128)(2,1)S(1)}, u32[]{:S(2)}, u32[]{:S(2)}) collective-permute-start(bf16[5,48,1,128]{3,1,0,2:T(8,128)(2,1)S(1)} %get-tuple-element.243), channel_id=1, source_target_pairs={{0,1},{1,2},{2,3},{3,4},{4,5},{5,6},{6,7},{7,8},{8,9},{9,10},{10,1... | collective-permute-start | bytes 184328 | tf_op jit(solution)/shard_map/ppermute | solution.py:25
  209.2 1.3 copy.43
  210.5 4.4 %scatter-add.54 = f32[1,5,48,8,128]{4,3,2,1,0:T(8,128)} dynamic-update-slice(f32[1,5,48,8,128]{4,3,2,1,0:T(8,128)} %copy.43, f32[1,5,48,1,128]{4,3,2,1,0:T(1,128)S(1)} %bitcast.537, s32[]{:T(128)} %constant.322.clone.1, s32[]{:T(128)} %constant.322.clone.1, s32[]{:T(128)} %constant.322.clone.1, s32[]{:T(128)} %constant.327.clone.1, s32[]{:T(128)} %constant.322.clone.1) | dynamic-update-slice | bytes 245764 | tf_op jit(solution)/shard_map/scatter-add | solution.py:100
  214.9 2.6 multiply_reduce_fusion
  217.4 52.7 %all-reduce.221 = (f32[]{:T(128)}, f32[]{:T(128)}) all-reduce(f32[]{:T(128)S(6)} %add.910, f32[]{:T(128)} %multiply_reduce_fusion), channel_id=1, replica_groups=mesh['tm'=2,'space'=16] {'tm','space'}, use_global_device_ids=true, to_apply=%region_3.4 | all-reduce | flops 2 | bytes 16 | tf_op jit(solution)/shard_map/psum | solution.py:157
  271.4 3.6 %multiply_subtract_fusion = f32[2,5,48,8,128]{4,3,2,1,0:T(8,128)} fusion(f32[2,5,48,8,128]{4,3,2,1,0:T(8,128)} %param.26, f32[]{:T(128)S(6)} %div.69, f32[2,2,48,8,128]{4,3,2,1,0:T(8,128)} %bitcast.530, f32[2,5,48,8,128]{4,3,2,1,0:T(8,128)S(1)} %copy-done.1, f32[1,5,48,8,128]{4,3,2,1,0:T(8,128)} %scatter-add.54, f32[1,5,48,8,128]{4,3,2,1,0:T(8,128)S(1)} %copy.44), kind=kLoop, calls=%fused_computation.7 | loop fusion | flops 2457600 | bytes 8650756 | tf_op jit(solution)/shard_map/sub | solution.py:182
  (251 shorter events, 25.7 us)
Async XLA Ops:
  3.8 3.3 %copy-start.8 = (f32[5,48,8,128]{3,1,2,0:T(8,128)}, f32[5,48,8,128]{3,1,2,0:T(8,128)S(1)}, u32[]{:S(2)}) copy-start(f32[5,48,8,128]{3,1,2,0:T(8,128)S(1)} %get-tuple-element.131) | copy-start | bytes 2949124
  4.5 122.4 %collective-permute-start = (f32[5,48,1,128]{3,1,2,0:T(8,128)}, f32[5,48,1,128]{3,1,2,0:T(8,128)}, u32[]{:S(2)}, u32[]{:S(2)}) collective-permute-start(f32[5,48,1,128]{3,1,2,0:T(8,128)} %get-tuple-element.231), channel_id=1, source_target_pairs={{0,1},{1,2},{2,3},{3,4},{4,5},{5,6},{6,7},{7,8},{8,9},{9,10},{10,1... | collective-permute-start | bytes 368648 | tf_op jit(solution)/shard_map/ppermute | solution.py:25
  4.5 122.4 %collective-permute-start.1 = (f32[5,48,1,128]{3,1,2,0:T(8,128)}, f32[5,48,1,128]{3,1,2,0:T(8,128)}, u32[]{:S(2)}, u32[]{:S(2)}) collective-permute-start(f32[5,48,1,128]{3,1,2,0:T(8,128)} %get-tuple-element.232), channel_id=1, source_target_pairs={{1,0},{2,1},{3,2},{4,3},{5,4},{6,5},{7,6},{8,7},{9,8},{10,9},{11,1... | collective-permute-start | bytes 368648 | tf_op jit(solution)/shard_map/ppermute | solution.py:26
  7.0 121.1 %collective-permute-start.7 = (f32[5,48,1,128]{3,1,2,0:T(8,128)}, f32[5,48,1,128]{3,1,2,0:T(8,128)}, u32[]{:S(2)}, u32[]{:S(2)}) collective-permute-start(f32[5,48,1,128]{3,1,2,0:T(8,128)} %get-tuple-element.235), channel_id=1, source_target_pairs={{0,1},{1,2},{2,3},{3,4},{4,5},{5,6},{6,7},{7,8},{8,9},{9,10},{10,1... | collective-permute-start | bytes 368648 | tf_op jit(solution)/shard_map/ppermute | solution.py:25
  7.2 118.0 %collective-permute-start.2 = (bf16[2,2,2,48,1,128]{5,3,4,2,1,0:T(8,128)(2,1)S(1)}, bf16[2,2,2,48,1,128]{5,3,4,2,1,0:T(8,128)(2,1)S(1)}, u32[]{:S(2)}, u32[]{:S(2)}) collective-permute-start(bf16[2,2,2,48,1,128]{5,3,4,2,1,0:T(8,128)(2,1)S(1)} %get-tuple-element.237), channel_id=1, source_target_pairs={{0,1},{1,2},{2,3},{3,4},{4,5},{5,6},{6,7},{7,8},{8,9},{9,10},{10,1... | collective-permute-start | bytes 294920 | tf_op jit(solution)/shard_map/ppermute | solution.py:25
  9.8 116.0 %collective-permute-start.3 = (bf16[2,2,2,48,1,128]{5,3,4,2,1,0:T(8,128)(2,1)S(1)}, bf16[2,2,2,48,1,128]{5,3,4,2,1,0:T(8,128)(2,1)}, u32[]{:S(2)}, u32[]{:S(2)}) collective-permute-start(bf16[2,2,2,48,1,128]{5,3,4,2,1,0:T(8,128)(2,1)S(1)} %get-tuple-element.238), channel_id=1, source_target_pairs={{1,0},{2,1},{3,2},{4,3},{5,4},{6,5},{7,6},{8,7},{9,8},{10,9},{11,1... | collective-permute-start | bytes 294920 | tf_op jit(solution)/shard_map/ppermute | solution.py:26
  10.6 85.0 %copy-start.15 = (f32[2,2048]{1,0:T(2,128)S(1)}, f32[2,2048]{1,0:T(2,128)}, u32[]{:S(2)}) copy-start(f32[2,2048]{1,0:T(2,128)} %param.28) | copy-start | bytes 49156
  10.7 85.0 %copy-start.16 = (f32[2,2048]{1,0:T(2,128)S(1)}, f32[2,2048]{1,0:T(2,128)}, u32[]{:S(2)}) copy-start(f32[2,2048]{1,0:T(2,128)} %param.30) | copy-start | bytes 49156
  10.7 85.0 %copy-start.17 = (f32[2,2048]{1,0:T(2,128)S(1)}, f32[2,2048]{1,0:T(2,128)}, u32[]{:S(2)}) copy-start(f32[2,2048]{1,0:T(2,128)} %param.32) | copy-start | bytes 49156
  10.7 86.3 %copy-start.20 = (s32[2]{0:T(128)S(1)}, s32[2]{0:T(128)}, u32[]{:S(2)}) copy-start(s32[2]{0:T(128)} %constant.788) | copy-start | bytes 28
  10.7 86.4 %copy-start.21 = (s32[2]{0:T(128)S(1)}, s32[2]{0:T(128)}, u32[]{:S(2)}) copy-start(s32[2]{0:T(128)} %constant.791) | copy-start | bytes 28
  125.2 3.0 %collective-permute-start.8 = (f32[5,48,1,128]{3,1,2,0:T(8,128)}, f32[5,48,1,128]{3,1,2,0:T(8,128)S(1)}, u32[]{:S(2)}, u32[]{:S(2)}) collective-permute-start(f32[5,48,1,128]{3,1,2,0:T(8,128)} %get-tuple-element.236), channel_id=1, source_target_pairs={{1,0},{2,1},{3,2},{4,3},{5,4},{6,5},{7,6},{8,7},{9,8},{10,9},{11,1... | collective-permute-start | bytes 368648 | tf_op jit(solution)/shard_map/ppermute | solution.py:26
  131.9 8.1 %collective-permute-start.4 = (f32[5,48,1,128]{3,1,2,0:T(8,128)S(1)}, f32[5,48,1,128]{3,1,2,0:T(8,128)S(1)}, u32[]{:S(2)}, u32[]{:S(2)}) collective-permute-start(f32[5,48,1,128]{3,1,2,0:T(8,128)S(1)} %get-tuple-element.229), channel_id=1, source_target_pairs={{0,1},{1,2},{2,3},{3,4},{4,5},{5,6},{6,7},{7,8},{8,9},{9,10},{10,1... | collective-permute-start | bytes 368648 | tf_op jit(solution)/shard_map/ppermute | solution.py:25
  131.9 8.0 %collective-permute-start.5 = (f32[5,48,1,128]{3,1,2,0:T(8,128)S(1)}, f32[5,48,1,128]{3,1,2,0:T(8,128)S(1)}, u32[]{:S(2)}, u32[]{:S(2)}) collective-permute-start(f32[5,48,1,128]{3,1,2,0:T(8,128)S(1)} %get-tuple-element.230), channel_id=1, source_target_pairs={{1,0},{2,1},{3,2},{4,3},{5,4},{6,5},{7,6},{8,7},{9,8},{10,9},{11,1... | collective-permute-start | bytes 368648 | tf_op jit(solution)/shard_map/ppermute | solution.py:26
  136.5 3.7 %collective-permute-start.10 = (f32[5,48,1,128]{3,1,2,0:T(8,128)S(1)}, f32[5,48,1,128]{3,1,2,0:T(8,128)S(1)}, u32[]{:S(2)}, u32[]{:S(2)}) collective-permute-start(f32[5,48,1,128]{3,1,2,0:T(8,128)S(1)} %get-tuple-element.234), channel_id=1, source_target_pairs={{1,0},{2,1},{3,2},{4,3},{5,4},{6,5},{7,6},{8,7},{9,8},{10,9},{11,1... | collective-permute-start | bytes 368648 | tf_op jit(solution)/shard_map/ppermute | solution.py:26
  137.1 7.1 %collective-permute-start.9 = (f32[5,48,1,128]{3,1,2,0:T(8,128)S(1)}, f32[5,48,1,128]{3,1,2,0:T(8,128)S(1)}, u32[]{:S(2)}, u32[]{:S(2)}) collective-permute-start(f32[5,48,1,128]{3,1,2,0:T(8,128)S(1)} %get-tuple-element.233), channel_id=1, source_target_pairs={{0,1},{1,2},{2,3},{3,4},{4,5},{5,6},{6,7},{7,8},{8,9},{9,10},{10,1... | collective-permute-start | bytes 368648 | tf_op jit(solution)/shard_map/ppermute | solution.py:25
  145.7 10.4 %collective-permute-start.6 = (bf16[5,48,8,128]{3,1,2,0:T(8,128)(2,1)S(1)}, bf16[5,48,8,128]{3,1,2,0:T(8,128)(2,1)S(1)}, u32[]{:S(2)}, u32[]{:S(2)}) collective-permute-start(bf16[5,48,8,128]{3,1,2,0:T(8,128)(2,1)S(1)} %multiply_convert_fusion), channel_id=1, source_target_pairs={{0,16},{1,17},{2,18},{3,19},{4,20},{5,21},{6,22},{7,23},{8,24},{9,... | collective-permute-start | bytes 1474568 | tf_op jit(solution)/shard_map/ppermute | solution.py:34
  150.4 5.7 %copy-start.11 = (f32[2,5,48,8,128]{4,3,2,1,0:T(8,128)S(1)}, f32[2,5,48,8,128]{4,3,2,1,0:T(8,128)}, u32[]{:S(2)}) copy-start(f32[2,5,48,8,128]{4,3,2,1,0:T(8,128)} %param.29) | copy-start | bytes 5898244
  150.7 5.5 %copy-start.5 = (f32[2,5,48,8,128]{4,3,2,1,0:T(8,128)S(1)}, f32[2,5,48,8,128]{4,3,2,1,0:T(8,128)}, u32[]{:S(2)}) copy-start(f32[2,5,48,8,128]{4,3,2,1,0:T(8,128)} %param.27) | copy-start | bytes 5898244
  151.0 5.2 %copy-start.2 = (f32[2,5,48,8,128]{4,3,2,1,0:T(8,128)S(1)}, f32[2,5,48,8,128]{4,3,2,1,0:T(8,128)}, u32[]{:S(2)}) copy-start(f32[2,5,48,8,128]{4,3,2,1,0:T(8,128)} %param.26) | copy-start | bytes 5898244
  151.1 5.1 %copy-start.14 = (f32[5,48]{1,0:T(8,128)S(1)}, f32[5,48]{1,0:T(8,128)}, u32[]{:S(2)}) copy-start(f32[5,48]{1,0:T(8,128)} %param.31) | copy-start | bytes 2884
  163.0 19.7 %collective-permute-start.15 = (f32[5,48,8,128]{3,1,2,0:T(8,128)}, f32[5,48,8,128]{3,1,2,0:T(8,128)}, u32[]{:S(2)}, u32[]{:S(2)}) collective-permute-start(f32[5,48,8,128]{3,1,2,0:T(8,128)} %fusion.5), channel_id=1, source_target_pairs={{16,0},{17,1},{18,2},{19,3},{20,4},{21,5},{22,6},{23,7},{24,8},{25... | collective-permute-start | bytes 2949128 | tf_op jit(solution)/shard_map/ppermute | solution.py:34
  165.7 4.0 %copy-start.10 = (f32[5,48,10,128]{3,1,2,0:T(8,128)}, f32[5,48,10,128]{3,1,2,0:T(8,128)S(1)}, u32[]{:S(2)}) copy-start(f32[5,48,10,128]{3,1,2,0:T(8,128)S(1)} %get-tuple-element.106) | copy-start | bytes 3686404
  165.7 5.3 %collective-permute-start.11 = (bf16[5,48,1,128]{3,1,2,0:T(8,128)(2,1)S(1)}, bf16[5,48,1,128]{3,1,2,0:T(8,128)(2,1)S(1)}, u32[]{:S(2)}, u32[]{:S(2)}) collective-permute-start(bf16[5,48,1,128]{3,1,2,0:T(8,128)(2,1)S(1)} %get-tuple-element.241), channel_id=1, source_target_pairs={{0,1},{1,2},{2,3},{3,4},{4,5},{5,6},{6,7},{7,8},{8,9},{9,10},{10,1... | collective-permute-start | bytes 184328 | tf_op jit(solution)/shard_map/ppermute | solution.py:25
  165.8 5.3 %collective-permute-start.12 = (bf16[5,48,1,128]{3,1,2,0:T(8,128)(2,1)S(1)}, bf16[5,48,1,128]{3,1,2,0:T(8,128)(2,1)S(1)}, u32[]{:S(2)}, u32[]{:S(2)}) collective-permute-start(bf16[5,48,1,128]{3,1,2,0:T(8,128)(2,1)S(1)} %get-tuple-element.242), channel_id=1, source_target_pairs={{1,0},{2,1},{3,2},{4,3},{5,4},{6,5},{7,6},{8,7},{9,8},{10,9},{11,1... | collective-permute-start | bytes 184328 | tf_op jit(solution)/shard_map/ppermute | solution.py:26
  188.1 10.2 %collective-permute-start.16 = (bf16[5,48,1,128]{3,1,2,0:T(8,128)(2,1)S(1)}, bf16[5,48,1,128]{3,1,2,0:T(8,128)(2,1)S(1)}, u32[]{:S(2)}, u32[]{:S(2)}) collective-permute-start(bf16[5,48,1,128]{3,1,2,0:T(8,128)(2,1)S(1)} %get-tuple-element.245), channel_id=1, source_target_pairs={{0,1},{1,2},{2,3},{3,4},{4,5},{5,6},{6,7},{7,8},{8,9},{9,10},{10,1... | collective-permute-start | bytes 184328 | tf_op jit(solution)/shard_map/ppermute | solution.py:25
  188.1 10.3 %collective-permute-start.17 = (bf16[5,48,1,128]{3,1,2,0:T(8,128)(2,1)S(1)}, bf16[5,48,1,128]{3,1,2,0:T(8,128)(2,1)S(1)}, u32[]{:S(2)}, u32[]{:S(2)}) collective-permute-start(bf16[5,48,1,128]{3,1,2,0:T(8,128)(2,1)S(1)} %get-tuple-element.246), channel_id=1, source_target_pairs={{1,0},{2,1},{3,2},{4,3},{5,4},{6,5},{7,6},{8,7},{9,8},{10,9},{11,1... | collective-permute-start | bytes 184328 | tf_op jit(solution)/shard_map/ppermute | solution.py:26
  190.4 8.7 %collective-permute-start.13 = (bf16[5,48,1,128]{3,1,2,0:T(8,128)(2,1)S(1)}, bf16[5,48,1,128]{3,1,2,0:T(8,128)(2,1)S(1)}, u32[]{:S(2)}, u32[]{:S(2)}) collective-permute-start(bf16[5,48,1,128]{3,1,2,0:T(8,128)(2,1)S(1)} %get-tuple-element.239), channel_id=1, source_target_pairs={{0,1},{1,2},{2,3},{3,4},{4,5},{5,6},{6,7},{7,8},{8,9},{9,10},{10,1... | collective-permute-start | bytes 184328 | tf_op jit(solution)/shard_map/ppermute | solution.py:25
  198.2 3.4 %collective-permute-start.14 = (bf16[5,48,1,128]{3,1,2,0:T(8,128)(2,1)S(1)}, bf16[5,48,1,128]{3,1,2,0:T(8,128)(2,1)S(1)}, u32[]{:S(2)}, u32[]{:S(2)}) collective-permute-start(bf16[5,48,1,128]{3,1,2,0:T(8,128)(2,1)S(1)} %get-tuple-element.240), channel_id=1, source_target_pairs={{1,0},{2,1},{3,2},{4,3},{5,4},{6,5},{7,6},{8,7},{9,8},{10,9},{11,1... | collective-permute-start | bytes 184328 | tf_op jit(solution)/shard_map/ppermute | solution.py:26
  203.2 5.0 %collective-permute-start.18 = (bf16[5,48,1,128]{3,1,0,2:T(8,128)(2,1)S(1)}, bf16[5,48,1,128]{3,1,0,2:T(8,128)(2,1)S(1)}, u32[]{:S(2)}, u32[]{:S(2)}) collective-permute-start(bf16[5,48,1,128]{3,1,0,2:T(8,128)(2,1)S(1)} %get-tuple-element.243), channel_id=1, source_target_pairs={{0,1},{1,2},{2,3},{3,4},{4,5},{5,6},{6,7},{7,8},{8,9},{9,10},{10,1... | collective-permute-start | bytes 184328 | tf_op jit(solution)/shard_map/ppermute | solution.py:25
  207.3 1.9 collective-permute-start.19
  209.2 5.7 %copy-start.1 = (f32[2,5,48,8,128]{4,3,2,1,0:T(8,128)S(1)}, f32[2,5,48,8,128]{4,3,2,1,0:T(8,128)}, u32[]{:S(2)}) copy-start(f32[2,5,48,8,128]{4,3,2,1,0:T(8,128)} %copy-done) | copy-start | bytes 5898244
  (11 other events, 22.6 us)
where the time goes:
time: 276 us; the launch traced here: 275 us
  blocking collectives  103 us (37%)
  other arithmetic  60 us (22%)
  local copies, waits for them, and re-layouts  52.3 us (19%)
  starting transfers between devices  30.8 us (11%)
  waiting for transfers between devices  24.5 us (9%)
  between operations  4.8 us (2%)
    psum x1, blocking collectives, on_device(): misfit_square = lax.psum(misfit_local, ('tm', 'space'))  52.7 us
    psum x1, blocking collectives, on_device(): observed = lax.psum(local_values, 'space')  50 us
    gather x3, local copies, waits for them, and re-layouts, on_device(): jnp.take_along_axis(flattened, local_index, axis=1)  34.9 us
    unnamed x20, other arithmetic  31.8 us
    ppermute x9, starting transfers between devices, extended(): before = lax.ppermute(last, axis, up)  14.7 us
    ppermute x2, waiting for transfers between devices, shifted(): return lax.ppermute(shard, axis, pairs)  13.5 us
    ppermute x9, starting transfers between devices, extended(): after = lax.ppermute(first, axis, down)  10.5 us
    ppermute x9, waiting for transfers between devices, extended(): before = lax.ppermute(last, axis, up)  7.4 us
  transfers between devices with their start and end apart: 20, of which 9 were waited for; matrix products, arithmetic and copies ran while one was open for 28% of the time, Pallas kernels for 0%

commit v1 on v0

--- a/solution.py
+++ b/solution.py
@@ -148,7 +148,7 @@
     )
     flattened = increment[:, :2].reshape(subcount, 2 * levels * width * latitude)
     local_values = jnp.where(owned, jnp.take_along_axis(flattened, local_index, axis=1), 0.0)
-    observed = lax.psum(local_values, "space")
+    observed = jnp.sum(lax.all_gather(local_values, "space"), axis=0)
     sensor_residual = innovation - sensor_error * sensor_multiplier - observed
     sensor_next = sensor_multiplier + relaxation * sensor_residual
     misfit_local = jnp.sum(model_residual * model_residual) + jnp.sum(

time: 276 us -> 238 us (0.86)
  blocking collectives: 103 us -> 68.5 us
  starting transfers between devices: 30.8 us -> 22.3 us
  waiting for transfers between devices: 24.5 us -> 30.1 us
    psum x1 -> x0, blocking collectives: 50 us -> none  [on_device(): observed = lax.psum(local_values, 'space')]
    all_gather x0 -> x1, blocking collectives: none -> 19.8 us  [on_device(): observed = jnp.sum(lax.all_gather(local_values, 'space'), axis=0)]
    ppermute x9, starting transfers between devices: 14.7 us -> 7.36 us  [extended(): before = lax.ppermute(last, axis, up)]
    ppermute x2, waiting for transfers between devices: 13.5 us -> 20.4 us  [shifted(): return lax.ppermute(shard, axis, pairs)]
    psum x1, blocking collectives: 52.7 us -> 48.8 us  [on_device(): misfit_square = lax.psum(misfit_local, ('tm', 'space'))]
    unnamed x20 -> x21, other arithmetic: 31.8 us -> 31.9 us
  transfers between devices with their start and end apart: 20 -> 20, of which waited for: 9 -> 10; matrix products, arithmetic and copies ran while one was open for 28% -> 33% of each run, Pallas kernels for 0% -> 0%
where the time goes in v1:
time: 238 us
  blocking collectives  68.5 us (29%)
  other arithmetic  60.1 us (25%)
  local copies, waits for them, and re-layouts  52.1 us (22%)
  waiting for transfers between devices  30.1 us (13%)
  starting transfers between devices  22.3 us (9%)
  between operations  4.82 us (2%)
    psum x1, blocking collectives, on_device(): misfit_square = lax.psum(misfit_local, ('tm', 'space'))  48.8 us
    gather x3, local copies, waits for them, and re-layouts, on_device(): jnp.take_along_axis(flattened, local_index, axis=1)  34.9 us
    unnamed x21, other arithmetic  31.9 us
    ppermute x2, waiting for transfers between devices, shifted(): return lax.ppermute(shard, axis, pairs)  20.4 us
    all_gather x1, blocking collectives, on_device(): observed = jnp.sum(lax.all_gather(local_values, 'space'), axis=0)  19.8 us
    ppermute x9, starting transfers between devices, extended(): after = lax.ppermute(first, axis, down)  9.59 us
    ppermute x9, starting transfers between devices, extended(): before = lax.ppermute(last, axis, up)  7.36 us
    unnamed x51, local copies, waits for them, and re-layouts  6.66 us
  transfers between devices with their start and end apart: 20, of which 10 were waited for; matrix products, arithmetic and copies ran while one was open for 33% of the time, Pallas kernels for 0%

profile of v1, /device:TPU:12, one launch (start us, length us, event | category | flops | bytes accessed | tf_op | source)
XLA Modules:
  0.0 237.9 jit_solution(16596057230916992848)
XLA Ops:
  0.6 1.9 copy.52
  4.5 1.7 collective-permute-start.1
  7.2 2.6 %collective-permute-start.2 = (bf16[2,2,2,48,1,128]{5,3,4,2,1,0:T(8,128)(2,1)S(1)}, bf16[2,2,2,48,1,128]{5,3,4,2,1,0:T(8,128)(2,1)S(1)}, u32[]{:S(2)}, u32[]{:S(2)}) collective-permute-start(bf16[2,2,2,48,1,128]{5,3,4,2,1,0:T(8,128)(2,1)S(1)} %get-tuple-element.237), channel_id=1, source_target_pairs={{0,1},{1,2},{2,3},{3,4},{4,5},{5,6},{6,7},{7,8},{8,9},{9,10},{10,1... | collective-permute-start | bytes 294920 | tf_op jit(solution)/shard_map/ppermute | solution.py:25
  10.7 34.9 %gather_fusion = f32[4096]{0:T(1024)S(1)} fusion(f32[2,98304]{1,0:T(2,128)S(1)} %bitcast.528, s32[4096]{0:T(1024)S(1)} %bitcast.529), kind=kCustom, calls=%fused_computation | custom fusion | bytes 65536 | tf_op jit(solution)/shard_map/jit(take_along_axis)/gather | solution.py:150
  45.7 19.8 %all-gather.1 = f32[16,2,2048]{2,1,0:T(2,128)S(1)} all-gather(f32[1,2,2048]{2,1,0:T(2,128)S(1)} %fusion.204), channel_id=2, replica_groups=mesh['tm'=2,'space'=16] {'space'}, dimensions={0}, use_global_device_ids=true | all-gather | bytes 278528 | tf_op jit(solution)/shard_map/all_gather | solution.py:151
  65.6 1.3 select_bitcast_fusion.1
  67.1 27.9 %scatter_custom_fusion = f32[196608]{0:T(1024)} fusion(s32[4096]{0:T(1024)S(1)} %bitcast.543, f32[4096]{0:T(1024)S(1)} %bitcast.542, f32[]{:T(128)} %constant.307.clone.1), kind=kCustom, calls=%fused_computation.80 | custom fusion | flops 4096 | bytes 786436
  101.8 2.9 %collective-permute-start.4 = (f32[5,48,1,128]{3,1,2,0:T(8,128)S(1)}, f32[5,48,1,128]{3,1,2,0:T(8,128)S(1)}, u32[]{:S(2)}, u32[]{:S(2)}) collective-permute-start(f32[5,48,1,128]{3,1,2,0:T(8,128)S(1)} %get-tuple-element.229), channel_id=1, source_target_pairs={{0,1},{1,2},{2,3},{3,4},{4,5},{5,6},{6,7},{7,8},{8,9},{9,10},{10,1... | collective-permute-start | bytes 368648 | tf_op jit(solution)/shard_map/ppermute | solution.py:25
  104.7 1.9 collective-permute-start.10
  107.4 2.9 %collective-permute-done.10 = f32[5,48,1,128]{3,1,2,0:T(8,128)S(1)} collective-permute-done((f32[5,48,1,128]{3,1,2,0:T(8,128)S(1)}, f32[5,48,1,128]{3,1,2,0:T(8,128)S(1)}, u32[]{:S(2)}, u32[]{:S(2)}) %collective-permute-start.10) | collective-permute-done | bytes 122912 | tf_op jit(solution)/shard_map/ppermute | solution.py:26
  110.3 2.5 %collective-permute-done.9 = f32[5,48,1,128]{3,1,2,0:T(8,128)S(1)} collective-permute-done((f32[5,48,1,128]{3,1,2,0:T(8,128)S(1)}, f32[5,48,1,128]{3,1,2,0:T(8,128)S(1)}, u32[]{:S(2)}, u32[]{:S(2)}) %collective-permute-start.9) | collective-permute-done | bytes 122912 | tf_op jit(solution)/shard_map/ppermute | solution.py:25
  114.3 4.0 %collective-permute-start.6 = (bf16[5,48,8,128]{3,1,2,0:T(8,128)(2,1)S(1)}, bf16[5,48,8,128]{3,1,2,0:T(8,128)(2,1)S(1)}, u32[]{:S(2)}, u32[]{:S(2)}) collective-permute-start(bf16[5,48,8,128]{3,1,2,0:T(8,128)(2,1)S(1)} %multiply_convert_fusion), channel_id=1, source_target_pairs={{0,16},{1,17},{2,18},{3,19},{4,20},{5,21},{6,22},{7,23},{8,24},{9,... | collective-permute-start | bytes 1474568 | tf_op jit(solution)/shard_map/ppermute | solution.py:34
  119.4 7.9 %collective-permute-done.6 = bf16[5,48,8,128]{3,1,2,0:T(8,128)(2,1)S(1)} collective-permute-done((bf16[5,48,8,128]{3,1,2,0:T(8,128)(2,1)S(1)}, bf16[5,48,8,128]{3,1,2,0:T(8,128)(2,1)S(1)}, u32[]{:S(2)}, u32[]{:S(2)}) %collective-permute-start.6) | collective-permute-done | bytes 491552 | tf_op jit(solution)/shard_map/ppermute | solution.py:34
  127.5 1.6 broadcast_multiply_fusion
  131.6 1.4 copy-done.4
  133.0 1.2 fusion.5
  134.3 1.3 collective-permute-start.15
  137.1 1.7 collective-permute-start.12
  138.8 1.2 multiply_reduce_fusion.1
  142.3 1.6 fusion.200
  143.9 1.6 fusion.199
  145.5 12.5 %collective-permute-done.15 = f32[5,48,8,128]{3,1,2,0:T(8,128)} collective-permute-done((f32[5,48,8,128]{3,1,2,0:T(8,128)}, f32[5,48,8,128]{3,1,2,0:T(8,128)}, u32[]{:S(2)}, u32[]{:S(2)}) %collective-permute-start.15) | collective-permute-done | bytes 983072 | tf_op jit(solution)/shard_map/ppermute | solution.py:34
  158.0 1.7 broadcast_multiply_fusion.3
  163.4 1.7 collective-permute-start.17
  165.7 1.7 collective-permute-start.14
  171.3 1.7 collective-permute-start.18
  173.9 1.4 collective-permute-done.18
  175.9 1.3 copy.59
  177.3 4.4 %scatter-add.54 = f32[1,5,48,8,128]{4,3,2,1,0:T(8,128)} dynamic-update-slice(f32[1,5,48,8,128]{4,3,2,1,0:T(8,128)} %copy.59, f32[1,5,48,1,128]{4,3,2,1,0:T(1,128)S(1)} %bitcast.539, s32[]{:T(128)} %constant.322.clone.1, s32[]{:T(128)} %constant.322.clone.1, s32[]{:T(128)} %constant.322.clone.1, s32[]{:T(128)} %constant.327.clone.1, s32[]{:T(128)} %constant.322.clone.1) | dynamic-update-slice | bytes 245764 | tf_op jit(solution)/shard_map/scatter-add | solution.py:100
  181.6 2.6 %multiply_reduce_fusion = f32[]{:T(128)} fusion(f32[2,2,48,8,128]{4,3,2,1,0:T(8,128)} %bitcast.531, f32[2,5,48,8,128]{4,3,2,1,0:T(8,128)S(1)} %copy-done.1, f32[1,5,48,8,128]{4,3,2,1,0:T(8,128)} %scatter-add.54, f32[1,5,48,8,128]{4,3,2,1,0:T(8,128)S(1)} %copy.60), kind=kLoop, calls=%fused_computation.8 | loop fusion | flops 2457599 | bytes 4718596 | tf_op jit(solution)/shard_map/reduce_sum | solution.py:179
  184.2 48.8 %all-reduce.221 = (f32[]{:T(128)}, f32[]{:T(128)}) all-reduce(f32[]{:T(128)S(6)} %add.908, f32[]{:T(128)} %multiply_reduce_fusion), channel_id=1, replica_groups=mesh['tm'=2,'space'=16] {'tm','space'}, use_global_device_ids=true, to_apply=%region_3.4 | all-reduce | flops 2 | bytes 16 | tf_op jit(solution)/shard_map/psum | solution.py:157
  234.2 3.6 %multiply_subtract_fusion = f32[2,5,48,8,128]{4,3,2,1,0:T(8,128)} fusion(f32[2,5,48,8,128]{4,3,2,1,0:T(8,128)} %param.26, f32[]{:T(128)S(6)} %div.69, f32[2,2,48,8,128]{4,3,2,1,0:T(8,128)} %bitcast.532, f32[2,5,48,8,128]{4,3,2,1,0:T(8,128)S(1)} %copy-done.1, f32[1,5,48,8,128]{4,3,2,1,0:T(8,128)} %scatter-add.54, f32[1,5,48,8,128]{4,3,2,1,0:T(8,128)S(1)} %copy.60), kind=kLoop, calls=%fused_computation.7 | loop fusion | flops 2457600 | bytes 8650756 | tf_op jit(solution)/shard_map/sub | solution.py:182
  (252 shorter events, 27.8 us)
Async XLA Ops:
  3.8 3.3 %copy-start.8 = (f32[5,48,8,128]{3,1,2,0:T(8,128)}, f32[5,48,8,128]{3,1,2,0:T(8,128)S(1)}, u32[]{:S(2)}) copy-start(f32[5,48,8,128]{3,1,2,0:T(8,128)S(1)} %get-tuple-element.131) | copy-start | bytes 2949124
  4.5 92.3 %collective-permute-start = (f32[5,48,1,128]{3,1,2,0:T(8,128)}, f32[5,48,1,128]{3,1,2,0:T(8,128)}, u32[]{:S(2)}, u32[]{:S(2)}) collective-permute-start(f32[5,48,1,128]{3,1,2,0:T(8,128)} %get-tuple-element.231), channel_id=1, source_target_pairs={{0,1},{1,2},{2,3},{3,4},{4,5},{5,6},{6,7},{7,8},{8,9},{9,10},{10,1... | collective-permute-start | bytes 368648 | tf_op jit(solution)/shard_map/ppermute | solution.py:25
  4.5 92.3 %collective-permute-start.1 = (f32[5,48,1,128]{3,1,2,0:T(8,128)}, f32[5,48,1,128]{3,1,2,0:T(8,128)}, u32[]{:S(2)}, u32[]{:S(2)}) collective-permute-start(f32[5,48,1,128]{3,1,2,0:T(8,128)} %get-tuple-element.232), channel_id=1, source_target_pairs={{1,0},{2,1},{3,2},{4,3},{5,4},{6,5},{7,6},{8,7},{9,8},{10,9},{11,1... | collective-permute-start | bytes 368648 | tf_op jit(solution)/shard_map/ppermute | solution.py:26
  7.0 91.0 %collective-permute-start.7 = (f32[5,48,1,128]{3,1,2,0:T(8,128)}, f32[5,48,1,128]{3,1,2,0:T(8,128)}, u32[]{:S(2)}, u32[]{:S(2)}) collective-permute-start(f32[5,48,1,128]{3,1,2,0:T(8,128)} %get-tuple-element.235), channel_id=1, source_target_pairs={{0,1},{1,2},{2,3},{3,4},{4,5},{5,6},{6,7},{7,8},{8,9},{9,10},{10,1... | collective-permute-start | bytes 368648 | tf_op jit(solution)/shard_map/ppermute | solution.py:25
  7.2 87.9 %collective-permute-start.2 = (bf16[2,2,2,48,1,128]{5,3,4,2,1,0:T(8,128)(2,1)S(1)}, bf16[2,2,2,48,1,128]{5,3,4,2,1,0:T(8,128)(2,1)S(1)}, u32[]{:S(2)}, u32[]{:S(2)}) collective-permute-start(bf16[2,2,2,48,1,128]{5,3,4,2,1,0:T(8,128)(2,1)S(1)} %get-tuple-element.237), channel_id=1, source_target_pairs={{0,1},{1,2},{2,3},{3,4},{4,5},{5,6},{6,7},{7,8},{8,9},{9,10},{10,1... | collective-permute-start | bytes 294920 | tf_op jit(solution)/shard_map/ppermute | solution.py:25
  9.8 86.0 %collective-permute-start.3 = (bf16[2,2,2,48,1,128]{5,3,4,2,1,0:T(8,128)(2,1)S(1)}, bf16[2,2,2,48,1,128]{5,3,4,2,1,0:T(8,128)(2,1)}, u32[]{:S(2)}, u32[]{:S(2)}) collective-permute-start(bf16[2,2,2,48,1,128]{5,3,4,2,1,0:T(8,128)(2,1)S(1)} %get-tuple-element.238), channel_id=1, source_target_pairs={{1,0},{2,1},{3,2},{4,3},{5,4},{6,5},{7,6},{8,7},{9,8},{10,9},{11,1... | collective-permute-start | bytes 294920 | tf_op jit(solution)/shard_map/ppermute | solution.py:26
  10.6 54.9 %copy-start.15 = (f32[2,2048]{1,0:T(2,128)S(1)}, f32[2,2048]{1,0:T(2,128)}, u32[]{:S(2)}) copy-start(f32[2,2048]{1,0:T(2,128)} %param.28) | copy-start | bytes 49156
  10.7 54.9 %copy-start.16 = (f32[2,2048]{1,0:T(2,128)S(1)}, f32[2,2048]{1,0:T(2,128)}, u32[]{:S(2)}) copy-start(f32[2,2048]{1,0:T(2,128)} %param.30) | copy-start | bytes 49156
  10.7 54.9 %copy-start.17 = (f32[2,2048]{1,0:T(2,128)S(1)}, f32[2,2048]{1,0:T(2,128)}, u32[]{:S(2)}) copy-start(f32[2,2048]{1,0:T(2,128)} %param.32) | copy-start | bytes 49156
  10.7 56.2 %copy-start.20 = (s32[2]{0:T(128)S(1)}, s32[2]{0:T(128)}, u32[]{:S(2)}) copy-start(s32[2]{0:T(128)} %constant.788) | copy-start | bytes 28
  10.7 56.3 %copy-start.21 = (s32[2]{0:T(128)S(1)}, s32[2]{0:T(128)}, u32[]{:S(2)}) copy-start(s32[2]{0:T(128)} %constant.791) | copy-start | bytes 28
  95.1 3.1 %collective-permute-start.8 = (f32[5,48,1,128]{3,1,2,0:T(8,128)}, f32[5,48,1,128]{3,1,2,0:T(8,128)S(1)}, u32[]{:S(2)}, u32[]{:S(2)}) collective-permute-start(f32[5,48,1,128]{3,1,2,0:T(8,128)} %get-tuple-element.236), channel_id=1, source_target_pairs={{1,0},{2,1},{3,2},{4,3},{5,4},{6,5},{7,6},{8,7},{9,8},{10,9},{11,1... | collective-permute-start | bytes 368648 | tf_op jit(solution)/shard_map/ppermute | solution.py:26
  101.8 4.7 %collective-permute-start.4 = (f32[5,48,1,128]{3,1,2,0:T(8,128)S(1)}, f32[5,48,1,128]{3,1,2,0:T(8,128)S(1)}, u32[]{:S(2)}, u32[]{:S(2)}) collective-permute-start(f32[5,48,1,128]{3,1,2,0:T(8,128)S(1)} %get-tuple-element.229), channel_id=1, source_target_pairs={{0,1},{1,2},{2,3},{3,4},{4,5},{5,6},{6,7},{7,8},{8,9},{9,10},{10,1... | collective-permute-start | bytes 368648 | tf_op jit(solution)/shard_map/ppermute | solution.py:25
  104.7 2.4 %collective-permute-start.5 = (f32[5,48,1,128]{3,1,2,0:T(8,128)S(1)}, f32[5,48,1,128]{3,1,2,0:T(8,128)S(1)}, u32[]{:S(2)}, u32[]{:S(2)}) collective-permute-start(f32[5,48,1,128]{3,1,2,0:T(8,128)S(1)} %get-tuple-element.230), channel_id=1, source_target_pairs={{1,0},{2,1},{3,2},{4,3},{5,4},{6,5},{7,6},{8,7},{9,8},{10,9},{11,1... | collective-permute-start | bytes 368648 | tf_op jit(solution)/shard_map/ppermute | solution.py:26
  104.7 5.6 %collective-permute-start.10 = (f32[5,48,1,128]{3,1,2,0:T(8,128)S(1)}, f32[5,48,1,128]{3,1,2,0:T(8,128)S(1)}, u32[]{:S(2)}, u32[]{:S(2)}) collective-permute-start(f32[5,48,1,128]{3,1,2,0:T(8,128)S(1)} %get-tuple-element.234), channel_id=1, source_target_pairs={{1,0},{2,1},{3,2},{4,3},{5,4},{6,5},{7,6},{8,7},{9,8},{10,9},{11,1... | collective-permute-start | bytes 368648 | tf_op jit(solution)/shard_map/ppermute | solution.py:26
  106.6 6.2 %collective-permute-start.9 = (f32[5,48,1,128]{3,1,2,0:T(8,128)S(1)}, f32[5,48,1,128]{3,1,2,0:T(8,128)S(1)}, u32[]{:S(2)}, u32[]{:S(2)}) collective-permute-start(f32[5,48,1,128]{3,1,2,0:T(8,128)S(1)} %get-tuple-element.233), channel_id=1, source_target_pairs={{0,1},{1,2},{2,3},{3,4},{4,5},{5,6},{6,7},{7,8},{8,9},{9,10},{10,1... | collective-permute-start | bytes 368648 | tf_op jit(solution)/shard_map/ppermute | solution.py:25
  114.3 13.1 %collective-permute-start.6 = (bf16[5,48,8,128]{3,1,2,0:T(8,128)(2,1)S(1)}, bf16[5,48,8,128]{3,1,2,0:T(8,128)(2,1)S(1)}, u32[]{:S(2)}, u32[]{:S(2)}) collective-permute-start(bf16[5,48,8,128]{3,1,2,0:T(8,128)(2,1)S(1)} %multiply_convert_fusion), channel_id=1, source_target_pairs={{0,16},{1,17},{2,18},{3,19},{4,20},{5,21},{6,22},{7,23},{8,24},{9,... | collective-permute-start | bytes 1474568 | tf_op jit(solution)/shard_map/ppermute | solution.py:34
  118.8 8.6 %copy-start.11 = (f32[2,5,48,8,128]{4,3,2,1,0:T(8,128)S(1)}, f32[2,5,48,8,128]{4,3,2,1,0:T(8,128)}, u32[]{:S(2)}) copy-start(f32[2,5,48,8,128]{4,3,2,1,0:T(8,128)} %param.29) | copy-start | bytes 5898244
  119.0 8.4 %copy-start.5 = (f32[2,5,48,8,128]{4,3,2,1,0:T(8,128)S(1)}, f32[2,5,48,8,128]{4,3,2,1,0:T(8,128)}, u32[]{:S(2)}) copy-start(f32[2,5,48,8,128]{4,3,2,1,0:T(8,128)} %param.27) | copy-start | bytes 5898244
  119.3 8.1 %copy-start.2 = (f32[2,5,48,8,128]{4,3,2,1,0:T(8,128)S(1)}, f32[2,5,48,8,128]{4,3,2,1,0:T(8,128)}, u32[]{:S(2)}) copy-start(f32[2,5,48,8,128]{4,3,2,1,0:T(8,128)} %param.26) | copy-start | bytes 5898244
  119.4 8.0 %copy-start.14 = (f32[5,48]{1,0:T(8,128)S(1)}, f32[5,48]{1,0:T(8,128)}, u32[]{:S(2)}) copy-start(f32[5,48]{1,0:T(8,128)} %param.31) | copy-start | bytes 2884
  134.3 23.7 %collective-permute-start.15 = (f32[5,48,8,128]{3,1,2,0:T(8,128)}, f32[5,48,8,128]{3,1,2,0:T(8,128)}, u32[]{:S(2)}, u32[]{:S(2)}) collective-permute-start(f32[5,48,8,128]{3,1,2,0:T(8,128)} %fusion.5), channel_id=1, source_target_pairs={{16,0},{17,1},{18,2},{19,3},{20,4},{21,5},{22,6},{23,7},{24,8},{25... | collective-permute-start | bytes 2949128 | tf_op jit(solution)/shard_map/ppermute | solution.py:34
  137.0 4.0 %copy-start.10 = (f32[5,48,10,128]{3,1,2,0:T(8,128)}, f32[5,48,10,128]{3,1,2,0:T(8,128)S(1)}, u32[]{:S(2)}) copy-start(f32[5,48,10,128]{3,1,2,0:T(8,128)S(1)} %get-tuple-element.106) | copy-start | bytes 3686404
  137.0 5.3 %collective-permute-start.11 = (bf16[5,48,1,128]{3,1,2,0:T(8,128)(2,1)S(1)}, bf16[5,48,1,128]{3,1,2,0:T(8,128)(2,1)S(1)}, u32[]{:S(2)}, u32[]{:S(2)}) collective-permute-start(bf16[5,48,1,128]{3,1,2,0:T(8,128)(2,1)S(1)} %get-tuple-element.241), channel_id=1, source_target_pairs={{0,1},{1,2},{2,3},{3,4},{4,5},{5,6},{6,7},{7,8},{8,9},{9,10},{10,1... | collective-permute-start | bytes 184328 | tf_op jit(solution)/shard_map/ppermute | solution.py:25
  137.1 5.3 %collective-permute-start.12 = (bf16[5,48,1,128]{3,1,2,0:T(8,128)(2,1)S(1)}, bf16[5,48,1,128]{3,1,2,0:T(8,128)(2,1)S(1)}, u32[]{:S(2)}, u32[]{:S(2)}) collective-permute-start(bf16[5,48,1,128]{3,1,2,0:T(8,128)(2,1)S(1)} %get-tuple-element.242), channel_id=1, source_target_pairs={{1,0},{2,1},{3,2},{4,3},{5,4},{6,5},{7,6},{8,7},{9,8},{10,9},{11,1... | collective-permute-start | bytes 184328 | tf_op jit(solution)/shard_map/ppermute | solution.py:26
  163.3 4.2 %collective-permute-start.16 = (bf16[5,48,1,128]{3,1,2,0:T(8,128)(2,1)S(1)}, bf16[5,48,1,128]{3,1,2,0:T(8,128)(2,1)S(1)}, u32[]{:S(2)}, u32[]{:S(2)}) collective-permute-start(bf16[5,48,1,128]{3,1,2,0:T(8,128)(2,1)S(1)} %get-tuple-element.245), channel_id=1, source_target_pairs={{0,1},{1,2},{2,3},{3,4},{4,5},{5,6},{6,7},{7,8},{8,9},{9,10},{10,1... | collective-permute-start | bytes 184328 | tf_op jit(solution)/shard_map/ppermute | solution.py:25
  163.4 4.1 %collective-permute-start.17 = (bf16[5,48,1,128]{3,1,2,0:T(8,128)(2,1)S(1)}, bf16[5,48,1,128]{3,1,2,0:T(8,128)(2,1)S(1)}, u32[]{:S(2)}, u32[]{:S(2)}) collective-permute-start(bf16[5,48,1,128]{3,1,2,0:T(8,128)(2,1)S(1)} %get-tuple-element.246), channel_id=1, source_target_pairs={{1,0},{2,1},{3,2},{4,3},{5,4},{6,5},{7,6},{8,7},{9,8},{10,9},{11,1... | collective-permute-start | bytes 184328 | tf_op jit(solution)/shard_map/ppermute | solution.py:26
  165.6 3.7 %collective-permute-start.13 = (bf16[5,48,1,128]{3,1,2,0:T(8,128)(2,1)S(1)}, bf16[5,48,1,128]{3,1,2,0:T(8,128)(2,1)S(1)}, u32[]{:S(2)}, u32[]{:S(2)}) collective-permute-start(bf16[5,48,1,128]{3,1,2,0:T(8,128)(2,1)S(1)} %get-tuple-element.239), channel_id=1, source_target_pairs={{0,1},{1,2},{2,3},{3,4},{4,5},{5,6},{6,7},{7,8},{8,9},{9,10},{10,1... | collective-permute-start | bytes 184328 | tf_op jit(solution)/shard_map/ppermute | solution.py:25
  165.7 4.0 %collective-permute-start.14 = (bf16[5,48,1,128]{3,1,2,0:T(8,128)(2,1)S(1)}, bf16[5,48,1,128]{3,1,2,0:T(8,128)(2,1)S(1)}, u32[]{:S(2)}, u32[]{:S(2)}) collective-permute-start(bf16[5,48,1,128]{3,1,2,0:T(8,128)(2,1)S(1)} %get-tuple-element.240), channel_id=1, source_target_pairs={{1,0},{2,1},{3,2},{4,3},{5,4},{6,5},{7,6},{8,7},{9,8},{10,9},{11,1... | collective-permute-start | bytes 184328 | tf_op jit(solution)/shard_map/ppermute | solution.py:26
  171.3 4.1 %collective-permute-start.18 = (bf16[5,48,1,128]{3,1,0,2:T(8,128)(2,1)S(1)}, bf16[5,48,1,128]{3,1,0,2:T(8,128)(2,1)S(1)}, u32[]{:S(2)}, u32[]{:S(2)}) collective-permute-start(bf16[5,48,1,128]{3,1,0,2:T(8,128)(2,1)S(1)} %get-tuple-element.243), channel_id=1, source_target_pairs={{0,1},{1,2},{2,3},{3,4},{4,5},{5,6},{6,7},{7,8},{8,9},{9,10},{10,1... | collective-permute-start | bytes 184328 | tf_op jit(solution)/shard_map/ppermute | solution.py:25
  173.0 2.9 %collective-permute-start.19 = (bf16[5,48,1,128]{3,1,0,2:T(8,128)(2,1)S(1)}, bf16[5,48,1,128]{3,1,0,2:T(8,128)(2,1)S(1)}, u32[]{:S(2)}, u32[]{:S(2)}) collective-permute-start(bf16[5,48,1,128]{3,1,0,2:T(8,128)(2,1)S(1)} %get-tuple-element.244), channel_id=1, source_target_pairs={{1,0},{2,1},{3,2},{4,3},{5,4},{6,5},{7,6},{8,7},{9,8},{10,9},{11,1... | collective-permute-start | bytes 184328 | tf_op jit(solution)/shard_map/ppermute | solution.py:26
  175.9 5.7 %copy-start.1 = (f32[2,5,48,8,128]{4,3,2,1,0:T(8,128)S(1)}, f32[2,5,48,8,128]{4,3,2,1,0:T(8,128)}, u32[]{:S(2)}) copy-start(f32[2,5,48,8,128]{4,3,2,1,0:T(8,128)} %copy-done) | copy-start | bytes 5898244
  (11 other events, 22.6 us)
